TPU v7x, 32 devices: a whole 2x2x4 slice. The times are simulated.
32 devices in a mesh: gx: 4 (over y, core), gy: 8 (over z, x).
Axes of the slice: x: 2, y: 2, z: 4, core: 2. Of those that a mesh axis runs over, the one named last changes fastest.
Arguments:
- velocity: float32 [3, 32, 64, 128], P(None, 'gx', 'gy'), may hold values from -2 to 2
- pressure: float32 [32, 64, 128], P('gx', 'gy'), may hold values from -6 to 6
- buoyancy: float32 [32, 64, 128], P('gx', 'gy'), may hold values from -6 to 6
- background: float32 [32, 64, 128], P('gx', 'gy'), may hold values from -0.7 to 0.7
- marker_value: float32 [8192, 256], P(('gx', 'gy')), may hold values from -2.5 to 2.5
- marker_height: float32 [8192, 256], P(('gx', 'gy')), may hold values from 0 to 127
- marker_owner: int32 [8192, 1], P(('gx', 'gy')), may hold values from 0 to 31; in each aligned block of 256 rows (0 to 255, 256 to 511, ...) at most 16 rows name the same one
- marker_column: int32 [8192], P(('gx', 'gy')), may hold values from 0 to 63
- block_count: int32 [32], P(('gx', 'gy')), may hold values from 1 to 256, 6144 in all
Outputs:
- new_velocity: float32 [3, 32, 64, 128], P(None, 'gx', 'gy')
- new_pressure: float32 [32, 64, 128], P('gx', 'gy')
- viscosity: float32 [32, 64, 128], P('gx', 'gy')
Inputs may be any that keep to these rules, and one draw needn't show every extreme that they name: `marker_owner`: among the 256 blocks of one device at most 16 name the same owner, and for some owner exactly 16 do. A device's live blocks are its first block_count ones; some device has all 256 live.
All inputs are finite; a program needn't handle non-finite values.
Results may differ from a plain program's by a relative error of at most 0.0003.
Values sent between devices are 32-bit elements; how exact they have to be, the bound alone decides.
No kernel may reach another device: no remote copies, remote signals or barrier semaphores. Data moves between devices by JAX's collectives and lax.ppermute only.
A program may use at most 64 MiB of HBM per device.

v0:
```python
import jax
import jax.numpy as jnp
from jax import lax
from jax.sharding import PartitionSpec as P

ITERS = 2
PRESS_STEP = 0.5
VEL_STEP = 0.05
DAMPING = 0.8


def extended(x, sides, width):
    for axis, dim in sides:
        devices, length = (lax.axis_size(axis), x.shape[dim])
        up = [(i, (i + 1) % devices) for i in range(devices - 1)]
        down = [(j, i) for i, j in up]
        last = lax.slice_in_dim(x, length - width, length, axis=dim)
        first = lax.slice_in_dim(x, 0, width, axis=dim)
        before = lax.ppermute(last, axis, up)
        after = lax.ppermute(first, axis, down)
        x = jnp.concatenate([before, x, after], axis=dim)
    return x


def inner_of(field):
    return field[..., 1:-1, 1:-1, :]


def east_of(field):
    return field[..., 2:, 1:-1, :]


def west_of(field):
    return field[..., :-2, 1:-1, :]


def north_of(field):
    return field[..., 1:-1, 2:, :]


def south_of(field):
    return field[..., 1:-1, :-2, :]


def upper_of(field):
    return jnp.concatenate([field[..., 1:], jnp.zeros_like(field[..., :1])], axis=-1)


def lower_of(field):
    return jnp.concatenate([jnp.zeros_like(field[..., :1]), field[..., :-1]], axis=-1)


def column_profile(values, heights, num_levels):
    lower_f = jnp.minimum(jnp.floor(heights), num_levels - 2.0)
    fraction = heights - lower_f
    lower_idx = lower_f.astype(jnp.int32)
    levels = jnp.arange(num_levels, dtype=jnp.int32)
    at_low = lower_idx[..., None] == levels
    at_up = (lower_idx + 1)[..., None] == levels
    weight = jnp.where(at_low, (1.0 - fraction)[..., None], 0.0) + jnp.where(
        at_up, fraction[..., None], 0.0
    )
    value_sum = jnp.sum(weight * values[..., None], axis=1)
    weight_sum = jnp.sum(weight, axis=1)
    return jnp.stack([value_sum, weight_sum], axis=1)


def place_rows(rows, profile, total_rows):
    one_hot = (jnp.arange(total_rows, dtype=jnp.int32)[:, None] == rows[None, :]).astype(
        jnp.float32
    )
    flat = profile.reshape(profile.shape[0], -1)
    return jnp.dot(
        one_hot, flat, precision=lax.Precision.HIGHEST, preferred_element_type=jnp.float32
    )


def stresses(vel_pad, visc_pad, pressure):
    vel_x = inner_of(vel_pad[0])
    vel_y = inner_of(vel_pad[1])
    vel_z = inner_of(vel_pad[2])
    visc = inner_of(visc_pad)
    grad_xx = vel_x - west_of(vel_pad[0])
    grad_yy = vel_y - south_of(vel_pad[1])
    grad_zz = vel_z - lower_of(vel_z)
    divergence = grad_xx + grad_yy + grad_zz
    new_press = pressure - PRESS_STEP * visc * divergence
    third = divergence / 3.0
    sig_xx = 2.0 * visc * (grad_xx - third) - new_press
    sig_yy = 2.0 * visc * (grad_yy - third) - new_press
    sig_zz = 2.0 * visc * (grad_zz - third) - new_press
    corner_xy = 0.25 * (visc + east_of(visc_pad) + north_of(visc_pad) + visc_pad[..., 2:, 2:, :])
    side_x = visc + east_of(visc_pad)
    side_y = visc + north_of(visc_pad)
    corner_xz = 0.25 * (side_x + upper_of(side_x))
    corner_yz = 0.25 * (side_y + upper_of(side_y))
    tau_xy = corner_xy * (north_of(vel_pad[0]) - vel_x + east_of(vel_pad[1]) - vel_y)
    tau_xz = corner_xz * (upper_of(vel_x) - vel_x + east_of(vel_pad[2]) - vel_z)
    tau_yz = corner_yz * (upper_of(vel_y) - vel_y + north_of(vel_pad[2]) - vel_z)
    return (new_press, jnp.stack([sig_xx, sig_yy, tau_xy, tau_xz, tau_yz]), sig_zz)


def residuals(stress_pad, sig_zz, buoyancy):
    sig_xx = stress_pad[0]
    sig_yy = stress_pad[1]
    tau_xy = stress_pad[2]
    tau_xz = stress_pad[3]
    tau_yz = stress_pad[4]
    mid_xz = inner_of(tau_xz)
    mid_yz = inner_of(tau_yz)
    res_x = (
        east_of(sig_xx)
        - inner_of(sig_xx)
        + inner_of(tau_xy)
        - south_of(tau_xy)
        + mid_xz
        - lower_of(mid_xz)
    )
    res_y = (
        inner_of(tau_xy)
        - west_of(tau_xy)
        + north_of(sig_yy)
        - inner_of(sig_yy)
        + mid_yz
        - lower_of(mid_yz)
    )
    res_z = (
        mid_xz - west_of(tau_xz) + mid_yz - south_of(tau_yz) + upper_of(sig_zz) - sig_zz + buoyancy
    )
    return jnp.stack([res_x, res_y, res_z])


def advance(vel, moment, residual, visc_pad, masks):
    visc = inner_of(visc_pad)
    faces = jnp.stack(
        [
            0.5 * (visc + east_of(visc_pad)),
            0.5 * (visc + north_of(visc_pad)),
            0.5 * (visc + upper_of(visc)),
        ]
    )
    moment = DAMPING * moment + residual
    vel = masks * (vel + VEL_STEP * moment / faces)
    return (vel, moment)


def rims(field):
    return extended(field, (("gx", 1), ("gy", 2)), 1)


def shards(
    velocity,
    pressure,
    buoyancy,
    background,
    marker_value,
    marker_height,
    marker_owner,
    marker_column,
    block_count,
):
    cells_x, cells_y, num_levels = pressure.shape
    block_rows = marker_owner.shape[0]
    size_x = lax.axis_size("gx")
    size_y = lax.axis_size("gy")
    devices = size_x * size_y
    capacity = max(2, (2 * block_rows + devices - 1) // devices)
    columns_n = cells_x * cells_y
    owner = marker_owner[:, 0]
    live = jnp.arange(block_rows) < block_count[0]
    hits = ((owner[:, None] == jnp.arange(devices)[None, :]) & live[:, None]).astype(jnp.int32)
    ranks = jnp.sum((jnp.cumsum(hits, axis=0) - 1) * hits, axis=1)
    slots = jnp.where(live, owner * capacity + ranks, devices * capacity)
    slot_hot = jnp.arange(devices * capacity, dtype=jnp.int32)[:, None] == slots[None, :]
    col_buffer = jnp.sum(jnp.where(slot_hot, (marker_column + 1)[None, :], 0), axis=1) - 1
    col_buffer = col_buffer.reshape(size_x, size_y, capacity)
    slot_matrix = slot_hot.astype(jnp.float32)
    payload = jnp.stack([marker_value, marker_height], axis=1)
    marks = payload.shape[2]
    send_buf = jnp.dot(
        slot_matrix,
        payload.reshape(block_rows, 2 * marks),
        precision=lax.Precision.HIGHEST,
        preferred_element_type=jnp.float32,
    )
    send_buf = send_buf.reshape(size_x, size_y, capacity, 2, marks)
    arrived, arrived_cols = (
        lax.all_to_all(
            lax.all_to_all(send_buf, "gx", split_axis=0, concat_axis=0, tiled=True),
            "gy",
            split_axis=1,
            concat_axis=1,
            tiled=True,
        ),
        lax.all_to_all(
            lax.all_to_all(col_buffer, "gx", split_axis=0, concat_axis=0, tiled=True),
            "gy",
            split_axis=1,
            concat_axis=1,
            tiled=True,
        ),
    )
    arrived = arrived.reshape(devices * capacity, 2, marks)
    arrived_cols = arrived_cols.reshape(devices * capacity)
    rows = jnp.where(arrived_cols >= 0, arrived_cols, columns_n).astype(jnp.int32)
    profile = column_profile(arrived[:, 0], arrived[:, 1], num_levels)
    sums = place_rows(rows, profile, columns_n)
    sums = sums.reshape(cells_x, cells_y, 2, num_levels)
    viscosity = jnp.exp((sums[:, :, 0] + background) / (sums[:, :, 1] + 1.0))
    global_x = lax.axis_index("gx") * cells_x + jnp.arange(cells_x)
    global_y = lax.axis_index("gy") * cells_y + jnp.arange(cells_y)
    mask_x = (global_x < cells_x * size_x - 1).astype(jnp.float32)
    mask_y = (global_y < cells_y * size_y - 1).astype(jnp.float32)
    mask_z = (jnp.arange(num_levels) < num_levels - 1).astype(jnp.float32)
    ones_grid = jnp.ones((cells_x, cells_y, num_levels), jnp.float32)
    masks = jnp.stack(
        [
            ones_grid * mask_x[:, None, None],
            ones_grid * mask_y[None, :, None],
            ones_grid * mask_z[None, None, :],
        ]
    )
    vel = velocity
    moment = jnp.zeros_like(velocity)
    visc_pad = rims(viscosity[None])[0]
    press = pressure
    for sweep_idx in range(ITERS):
        press, stress, sig_zz = stresses(rims(vel), visc_pad, press)
        residual = residuals(rims(stress), sig_zz, buoyancy)
        vel, moment = advance(vel, moment, residual, visc_pad, masks)
    return (vel, press, viscosity)


def solution(mesh):
    return jax.shard_map(
        shards,
        mesh=mesh,
        in_specs=(
            P(None, "gx", "gy", None),
            P("gx", "gy", None),
            P("gx", "gy", None),
            P("gx", "gy", None),
            P(("gx", "gy"), None),
            P(("gx", "gy"), None),
            P(("gx", "gy"), None),
            P(("gx", "gy")),
            P(("gx", "gy")),
        ),
        out_specs=(P(None, "gx", "gy", None), P("gx", "gy", None), P("gx", "gy", None)),
        check_vma=False,
    )
```

profile of v0, /device:TPU:1, one launch (start us, length us, event | category | flops | bytes accessed | tf_op | source)
XLA Modules:
  0.0 229.5 jit_solution(1652927440290417424)
XLA Ops:
  5.2 4.3 %all-to-all-start = ((s32[4,1,128]{2,1,0:T(1,128)}), s32[4,1,128]{2,1,0:T(1,128)S(1)}, u32[]{:S(2)}, u32[]{:S(2)}) async-start(s32[4,1,128]{2,1,0:T(1,128)} %reshape.171), calls=%async_computation | async-start | bytes 4096 | tf_op jit(solution)/shard_map/all_to_all | solution.py:196
  13.3 3.5 %all-to-all-start.2 = ((f32[4,8,16,2,256]{4,2,3,1,0:T(8,128)}), f32[4,8,16,2,256]{4,2,3,1,0:T(8,128)S(1)}, u32[]{:S(2)}, u32[]{:S(2)}) async-start(f32[4,8,16,2,256]{4,2,3,1,0:T(8,128)} %fusion.1), calls=%async_computation.2 | async-start | bytes 2097152 | tf_op jit(solution)/shard_map/all_to_all | solution.py:189
  18.7 11.7 %all-to-all-done.2 = f32[4,8,16,2,256]{4,2,3,1,0:T(8,128)S(1)} async-done(((f32[4,8,16,2,256]{4,2,3,1,0:T(8,128)}), f32[4,8,16,2,256]{4,2,3,1,0:T(8,128)S(1)}, u32[]{:S(2)}, u32[]{:S(2)}) %all-to-all-start.2) | async-done | bytes 1048608 | tf_op jit(solution)/shard_map/all_to_all | solution.py:189
  30.4 6.0 %all-to-all-start.1 = ((s32[4,8,16]{2,0,1:T(4,128)}), s32[4,8,16]{2,0,1:T(4,128)S(1)}, u32[]{:S(2)}, u32[]{:S(2)}) async-start(s32[4,8,16]{2,0,1:T(4,128)} %copy.41), calls=%async_computation.1 | async-start | bytes 32768 | tf_op jit(solution)/shard_map/all_to_all | solution.py:195
  37.4 4.4 %all-to-all-done.1 = s32[4,8,16]{2,0,1:T(4,128)S(1)} async-done(((s32[4,8,16]{2,0,1:T(4,128)}), s32[4,8,16]{2,0,1:T(4,128)S(1)}, u32[]{:S(2)}, u32[]{:S(2)}) %all-to-all-start.1) | async-done | bytes 2080 | tf_op jit(solution)/shard_map/all_to_all | solution.py:195
  41.8 3.6 %all-to-all-start.3 = ((f32[4,8,16,2,256]{4,2,3,0,1:T(8,128)}), f32[4,8,16,2,256]{4,2,3,0,1:T(8,128)S(1)}, u32[]{:S(2)}, u32[]{:S(2)}) async-start(f32[4,8,16,2,256]{4,2,3,0,1:T(8,128)} %copy.45), calls=%async_computation.3 | async-start | bytes 2097152 | tf_op jit(solution)/shard_map/all_to_all | solution.py:188
  45.4 4.2 %collective-permute-start.4 = (f32[3,1,8,128]{3,2,1,0:T(8,128)S(1)}, f32[3,1,8,128]{3,2,1,0:T(8,128)S(1)}, u32[]{:S(2)}, u32[]{:S(2)}) collective-permute-start(f32[3,1,8,128]{3,2,1,0:T(8,128)S(1)} %get-tuple-element.49), channel_id=1, source_target_pairs={{0,8},{8,16},{16,24},{1,9},{9,17},{17,25},{2,10},{10,18},{18,26},{... | collective-permute-start | bytes 36872 | tf_op jit(solution)/shard_map/ppermute | solution.py:19
  49.6 1.9 collective-permute-start.5
  51.7 3.2 %collective-permute-done.5 = f32[3,1,8,128]{3,2,1,0:T(8,128)S(1)} collective-permute-done((f32[3,1,8,128]{3,2,1,0:T(8,128)S(1)}, f32[3,1,8,128]{3,2,1,0:T(8,128)S(1)}, u32[]{:S(2)}, u32[]{:S(2)}) %collective-permute-start.5) | collective-permute-done | bytes 12320 | tf_op jit(solution)/shard_map/ppermute | solution.py:20
  54.9 3.5 %collective-permute-start.6 = (f32[3,10,1,128]{3,2,1,0:T(1,128)S(1)}, f32[3,10,1,128]{3,2,1,0:T(1,128)S(1)}, u32[]{:S(2)}, u32[]{:S(2)}) collective-permute-start(f32[3,10,1,128]{3,2,1,0:T(1,128)S(1)} %get-tuple-element.44), channel_id=1, source_target_pairs={{0,1},{1,2},{2,3},{3,4},{4,5},{5,6},{6,7},{8,9},{9,10},{10,11},{11... | collective-permute-start | bytes 46088 | tf_op jit(solution)/shard_map/ppermute | solution.py:19
  59.7 9.4 %all-to-all-done.3 = f32[4,8,16,2,256]{4,2,3,0,1:T(8,128)S(1)} async-done(((f32[4,8,16,2,256]{4,2,3,0,1:T(8,128)}), f32[4,8,16,2,256]{4,2,3,0,1:T(8,128)S(1)}, u32[]{:S(2)}, u32[]{:S(2)}) %all-to-all-start.3) | async-done | bytes 1048608 | tf_op jit(solution)/shard_map/all_to_all | solution.py:188
  69.4 91.5 %multiply_reduce_fusion = (f32[512,128]{1,0:T(8,128)S(1)}, f32[512,128]{1,0:T(8,128)S(1)}) fusion(f32[512,256]{1,0:T(8,128)S(1)} %slice_bitcast_fusion, f32[512,256]{1,0:T(8,128)S(1)} %get-tuple-element.17, s32[512,256]{1,0:T(8,128)S(1)} %broadcast_add_fusion, f32[512,256]{1,0:T(8,128)S(1)} %get-tuple-element.16, s32[512,256]{1,0:T(8,128)S(1)} %get-tuple-element.15), kind=kLoop, calls=%fused_computation | loop fusion | flops 134086656 | bytes 3145728 | tf_op jit(solution)/shard_map/reduce_sum | solution.py:63
  161.8 5.4 %collective-permute-start = (f32[1,1,8,128]{3,2,1,0:T(8,128)S(1)}, f32[1,1,8,128]{3,2,1,0:T(8,128)S(1)}, u32[]{:S(2)}, u32[]{:S(2)}) collective-permute-start(f32[1,1,8,128]{3,2,1,0:T(8,128)S(1)} %get-tuple-element.62), channel_id=1, source_target_pairs={{0,8},{8,16},{16,24},{1,9},{9,17},{17,25},{2,10},{10,18},{18,26},{... | collective-permute-start | bytes 12296 | tf_op jit(solution)/shard_map/ppermute | solution.py:19
  167.2 1.9 collective-permute-start.1
  169.2 2.9 %collective-permute-done.1 = f32[1,1,8,128]{3,2,1,0:T(8,128)S(1)} collective-permute-done((f32[1,1,8,128]{3,2,1,0:T(8,128)S(1)}, f32[1,1,8,128]{3,2,1,0:T(8,128)S(1)}, u32[]{:S(2)}, u32[]{:S(2)}) %collective-permute-start.1) | collective-permute-done | bytes 4128 | tf_op jit(solution)/shard_map/ppermute | solution.py:20
  172.2 2.7 %collective-permute-start.2 = (f32[1,10,1,128]{3,2,1,0:T(1,128)S(1)}, f32[1,10,1,128]{3,2,1,0:T(1,128)S(1)}, u32[]{:S(2)}, u32[]{:S(2)}) collective-permute-start(f32[1,10,1,128]{3,2,1,0:T(1,128)S(1)} %get-tuple-element.60), channel_id=1, source_target_pairs={{0,1},{1,2},{2,3},{3,4},{4,5},{5,6},{6,7},{8,9},{9,10},{10,11},{11... | collective-permute-start | bytes 15368 | tf_op jit(solution)/shard_map/ppermute | solution.py:19
  176.4 2.9 %collective-permute-done.3 = f32[1,10,1,128]{3,2,1,0:T(1,128)S(1)} collective-permute-done((f32[1,10,1,128]{3,2,1,0:T(1,128)S(1)}, f32[1,10,1,128]{3,2,1,0:T(1,128)S(1)}, u32[]{:S(2)}, u32[]{:S(2)}) %collective-permute-start.3) | collective-permute-done | bytes 5152 | tf_op jit(solution)/shard_map/ppermute | solution.py:20
  179.8 3.4 %collective-permute-start.8 = (f32[5,1,8,128]{3,2,1,0:T(8,128)S(1)}, f32[5,1,8,128]{3,2,1,0:T(8,128)S(1)}, u32[]{:S(2)}, u32[]{:S(2)}) collective-permute-start(f32[5,1,8,128]{3,2,1,0:T(8,128)S(1)} %get-tuple-element.40), channel_id=1, source_target_pairs={{0,8},{8,16},{16,24},{1,9},{9,17},{17,25},{2,10},{10,18},{18,26},{... | collective-permute-start | bytes 61448 | tf_op jit(solution)/shard_map/ppermute | solution.py:19
  183.2 1.9 collective-permute-start.9
  185.1 3.1 %collective-permute-done.9 = f32[5,1,8,128]{3,2,1,0:T(8,128)S(1)} collective-permute-done((f32[5,1,8,128]{3,2,1,0:T(8,128)S(1)}, f32[5,1,8,128]{3,2,1,0:T(8,128)S(1)}, u32[]{:S(2)}, u32[]{:S(2)}) %collective-permute-start.9) | collective-permute-done | bytes 20512 | tf_op jit(solution)/shard_map/ppermute | solution.py:20
  188.3 2.5 %collective-permute-start.10 = (f32[5,10,1,128]{3,2,1,0:T(1,128)S(1)}, f32[5,10,1,128]{3,2,1,0:T(1,128)S(1)}, u32[]{:S(2)}, u32[]{:S(2)}) collective-permute-start(f32[5,10,1,128]{3,2,1,0:T(1,128)S(1)} %get-tuple-element.36), channel_id=1, source_target_pairs={{0,1},{1,2},{2,3},{3,4},{4,5},{5,6},{6,7},{8,9},{9,10},{10,11},{11... | collective-permute-start | bytes 76808 | tf_op jit(solution)/shard_map/ppermute | solution.py:19
  192.3 3.2 %collective-permute-done.11 = f32[5,10,1,128]{3,2,1,0:T(1,128)S(1)} collective-permute-done((f32[5,10,1,128]{3,2,1,0:T(1,128)S(1)}, f32[5,10,1,128]{3,2,1,0:T(1,128)S(1)}, u32[]{:S(2)}, u32[]{:S(2)}) %collective-permute-start.11) | collective-permute-done | bytes 25632 | tf_op jit(solution)/shard_map/ppermute | solution.py:20
  195.9 3.4 %collective-permute-start.12 = (f32[3,1,8,128]{3,2,1,0:T(8,128)S(1)}, f32[3,1,8,128]{3,2,1,0:T(8,128)S(1)}, u32[]{:S(2)}, u32[]{:S(2)}) collective-permute-start(f32[3,1,8,128]{3,2,1,0:T(8,128)S(1)} %get-tuple-element.46), channel_id=1, source_target_pairs={{0,8},{8,16},{16,24},{1,9},{9,17},{17,25},{2,10},{10,18},{18,26},{... | collective-permute-start | bytes 36872 | tf_op jit(solution)/shard_map/ppermute | solution.py:19
  199.3 1.9 collective-permute-start.13
  201.2 3.1 %collective-permute-done.13 = f32[3,1,8,128]{3,2,1,0:T(8,128)S(1)} collective-permute-done((f32[3,1,8,128]{3,2,1,0:T(8,128)S(1)}, f32[3,1,8,128]{3,2,1,0:T(8,128)S(1)}, u32[]{:S(2)}, u32[]{:S(2)}) %collective-permute-start.13) | collective-permute-done | bytes 12320 | tf_op jit(solution)/shard_map/ppermute | solution.py:20
  204.3 2.5 %collective-permute-start.14 = (f32[3,10,1,128]{3,2,1,0:T(1,128)S(1)}, f32[3,10,1,128]{3,2,1,0:T(1,128)S(1)}, u32[]{:S(2)}, u32[]{:S(2)}) collective-permute-start(f32[3,10,1,128]{3,2,1,0:T(1,128)S(1)} %get-tuple-element.42), channel_id=1, source_target_pairs={{0,1},{1,2},{2,3},{3,4},{4,5},{5,6},{6,7},{8,9},{9,10},{10,11},{11... | collective-permute-start | bytes 46088 | tf_op jit(solution)/shard_map/ppermute | solution.py:19
  208.2 3.2 %collective-permute-done.15 = f32[3,10,1,128]{3,2,1,0:T(1,128)S(1)} collective-permute-done((f32[3,10,1,128]{3,2,1,0:T(1,128)S(1)}, f32[3,10,1,128]{3,2,1,0:T(1,128)S(1)}, u32[]{:S(2)}, u32[]{:S(2)}) %collective-permute-start.15) | collective-permute-done | bytes 15392 | tf_op jit(solution)/shard_map/ppermute | solution.py:20
  211.8 3.4 %collective-permute-start.16 = (f32[5,1,8,128]{3,2,1,0:T(8,128)S(1)}, f32[5,1,8,128]{3,2,1,0:T(8,128)S(1)}, u32[]{:S(2)}, u32[]{:S(2)}) collective-permute-start(f32[5,1,8,128]{3,2,1,0:T(8,128)S(1)} %get-tuple-element.38), channel_id=1, source_target_pairs={{0,8},{8,16},{16,24},{1,9},{9,17},{17,25},{2,10},{10,18},{18,26},{... | collective-permute-start | bytes 61448 | tf_op jit(solution)/shard_map/ppermute | solution.py:19
  215.2 1.9 collective-permute-start.17
  217.1 3.2 %collective-permute-done.17 = f32[5,1,8,128]{3,2,1,0:T(8,128)S(1)} collective-permute-done((f32[5,1,8,128]{3,2,1,0:T(8,128)S(1)}, f32[5,1,8,128]{3,2,1,0:T(8,128)S(1)}, u32[]{:S(2)}, u32[]{:S(2)}) %collective-permute-start.17) | collective-permute-done | bytes 20512 | tf_op jit(solution)/shard_map/ppermute | solution.py:20
  220.3 3.7 %collective-permute-start.18 = (f32[5,10,1,128]{3,2,1,0:T(1,128)S(1)}, f32[5,10,1,128]{3,2,1,0:T(1,128)S(1)}, u32[]{:S(2)}, u32[]{:S(2)}) collective-permute-start(f32[5,10,1,128]{3,2,1,0:T(1,128)S(1)} %get-tuple-element.34), channel_id=1, source_target_pairs={{0,1},{1,2},{2,3},{3,4},{4,5},{5,6},{6,7},{8,9},{9,10},{10,11},{11... | collective-permute-start | bytes 76808 | tf_op jit(solution)/shard_map/ppermute | solution.py:19
  225.5 3.1 %collective-permute-done.19 = f32[5,10,1,128]{3,2,1,0:T(1,128)S(1)} collective-permute-done((f32[5,10,1,128]{3,2,1,0:T(1,128)S(1)}, f32[5,10,1,128]{3,2,1,0:T(1,128)S(1)}, u32[]{:S(2)}, u32[]{:S(2)}) %collective-permute-start.19) | collective-permute-done | bytes 25632 | tf_op jit(solution)/shard_map/ppermute | solution.py:20
  (123 shorter events, 21.2 us)
Async XLA Ops:
  5.2 8.1 %all-to-all-start = ((s32[4,1,128]{2,1,0:T(1,128)}), s32[4,1,128]{2,1,0:T(1,128)S(1)}, u32[]{:S(2)}, u32[]{:S(2)}) async-start(s32[4,1,128]{2,1,0:T(1,128)} %reshape.171), calls=%async_computation | async-start | bytes 4096 | tf_op jit(solution)/shard_map/all_to_all | solution.py:196
  13.3 17.1 %all-to-all-start.2 = ((f32[4,8,16,2,256]{4,2,3,1,0:T(8,128)}), f32[4,8,16,2,256]{4,2,3,1,0:T(8,128)S(1)}, u32[]{:S(2)}, u32[]{:S(2)}) async-start(f32[4,8,16,2,256]{4,2,3,1,0:T(8,128)} %fusion.1), calls=%async_computation.2 | async-start | bytes 2097152 | tf_op jit(solution)/shard_map/all_to_all | solution.py:189
  30.4 11.4 %all-to-all-start.1 = ((s32[4,8,16]{2,0,1:T(4,128)}), s32[4,8,16]{2,0,1:T(4,128)S(1)}, u32[]{:S(2)}, u32[]{:S(2)}) async-start(s32[4,8,16]{2,0,1:T(4,128)} %copy.41), calls=%async_computation.1 | async-start | bytes 32768 | tf_op jit(solution)/shard_map/all_to_all | solution.py:195
  37.4 7.9 %copy-start = (f32[3,8,8,128]{3,2,1,0:T(8,128)S(1)}, f32[3,8,8,128]{3,2,1,0:T(8,128)}, u32[]{:S(2)}) copy-start(f32[3,8,8,128]{3,2,1,0:T(8,128)} %param.9) | copy-start | bytes 294916
  41.8 27.3 %all-to-all-start.3 = ((f32[4,8,16,2,256]{4,2,3,0,1:T(8,128)}), f32[4,8,16,2,256]{4,2,3,0,1:T(8,128)S(1)}, u32[]{:S(2)}, u32[]{:S(2)}) async-start(f32[4,8,16,2,256]{4,2,3,0,1:T(8,128)} %copy.45), calls=%async_computation.3 | async-start | bytes 2097152 | tf_op jit(solution)/shard_map/all_to_all | solution.py:188
  45.4 6.3 %collective-permute-start.4 = (f32[3,1,8,128]{3,2,1,0:T(8,128)S(1)}, f32[3,1,8,128]{3,2,1,0:T(8,128)S(1)}, u32[]{:S(2)}, u32[]{:S(2)}) collective-permute-start(f32[3,1,8,128]{3,2,1,0:T(8,128)S(1)} %get-tuple-element.49), channel_id=1, source_target_pairs={{0,8},{8,16},{16,24},{1,9},{9,17},{17,25},{2,10},{10,18},{18,26},{... | collective-permute-start | bytes 36872 | tf_op jit(solution)/shard_map/ppermute | solution.py:19
  49.6 5.3 %collective-permute-start.5 = (f32[3,1,8,128]{3,2,1,0:T(8,128)S(1)}, f32[3,1,8,128]{3,2,1,0:T(8,128)S(1)}, u32[]{:S(2)}, u32[]{:S(2)}) collective-permute-start(f32[3,1,8,128]{3,2,1,0:T(8,128)S(1)} %get-tuple-element.48), channel_id=1, source_target_pairs={{8,0},{16,8},{24,16},{9,1},{17,9},{25,17},{10,2},{18,10},{26,18},{... | collective-permute-start | bytes 36872 | tf_op jit(solution)/shard_map/ppermute | solution.py:20
  54.9 114.3 %collective-permute-start.6 = (f32[3,10,1,128]{3,2,1,0:T(1,128)S(1)}, f32[3,10,1,128]{3,2,1,0:T(1,128)S(1)}, u32[]{:S(2)}, u32[]{:S(2)}) collective-permute-start(f32[3,10,1,128]{3,2,1,0:T(1,128)S(1)} %get-tuple-element.44), channel_id=1, source_target_pairs={{0,1},{1,2},{2,3},{3,4},{4,5},{5,6},{6,7},{8,9},{9,10},{10,11},{11... | collective-permute-start | bytes 46088 | tf_op jit(solution)/shard_map/ppermute | solution.py:19
  58.4 110.7 %collective-permute-start.7 = (f32[3,10,1,128]{3,2,1,0:T(1,128)S(1)}, f32[3,10,1,128]{3,2,1,0:T(1,128)S(1)}, u32[]{:S(2)}, u32[]{:S(2)}) collective-permute-start(f32[3,10,1,128]{3,2,1,0:T(1,128)S(1)} %get-tuple-element.45), channel_id=1, source_target_pairs={{1,0},{2,1},{3,2},{4,3},{5,4},{6,5},{7,6},{9,8},{10,9},{11,10},{12... | collective-permute-start | bytes 46088 | tf_op jit(solution)/shard_map/ppermute | solution.py:20
  161.0 0.8 copy-start.4
  161.2 18.1 %copy-start.5 = (f32[8,8,128]{2,1,0:T(8,128)S(1)}, f32[8,8,128]{2,1,0:T(8,128)}, u32[]{:S(2)}) copy-start(f32[8,8,128]{2,1,0:T(8,128)} %param.10) | copy-start | bytes 98308
  161.8 17.7 %copy-start.1 = (f32[8,8,128]{2,1,0:T(8,128)}, f32[8,8,128]{2,1,0:T(8,128)S(1)}, u32[]{:S(2)}) copy-start(f32[8,8,128]{2,1,0:T(8,128)S(1)} %fusion.74) | copy-start | bytes 98308
  161.8 7.4 %collective-permute-start = (f32[1,1,8,128]{3,2,1,0:T(8,128)S(1)}, f32[1,1,8,128]{3,2,1,0:T(8,128)S(1)}, u32[]{:S(2)}, u32[]{:S(2)}) collective-permute-start(f32[1,1,8,128]{3,2,1,0:T(8,128)S(1)} %get-tuple-element.62), channel_id=1, source_target_pairs={{0,8},{8,16},{16,24},{1,9},{9,17},{17,25},{2,10},{10,18},{18,26},{... | collective-permute-start | bytes 12296 | tf_op jit(solution)/shard_map/ppermute | solution.py:19
  167.2 4.9 %collective-permute-start.1 = (f32[1,1,8,128]{3,2,1,0:T(8,128)S(1)}, f32[1,1,8,128]{3,2,1,0:T(8,128)S(1)}, u32[]{:S(2)}, u32[]{:S(2)}) collective-permute-start(f32[1,1,8,128]{3,2,1,0:T(8,128)S(1)} %get-tuple-element.63), channel_id=1, source_target_pairs={{8,0},{16,8},{24,16},{9,1},{17,9},{25,17},{10,2},{18,10},{26,18},{... | collective-permute-start | bytes 12296 | tf_op jit(solution)/shard_map/ppermute | solution.py:20
  172.2 4.2 %collective-permute-start.2 = (f32[1,10,1,128]{3,2,1,0:T(1,128)S(1)}, f32[1,10,1,128]{3,2,1,0:T(1,128)S(1)}, u32[]{:S(2)}, u32[]{:S(2)}) collective-permute-start(f32[1,10,1,128]{3,2,1,0:T(1,128)S(1)} %get-tuple-element.60), channel_id=1, source_target_pairs={{0,1},{1,2},{2,3},{3,4},{4,5},{5,6},{6,7},{8,9},{9,10},{10,11},{11... | collective-permute-start | bytes 15368 | tf_op jit(solution)/shard_map/ppermute | solution.py:19
  174.9 4.4 %collective-permute-start.3 = (f32[1,10,1,128]{3,2,1,0:T(1,128)S(1)}, f32[1,10,1,128]{3,2,1,0:T(1,128)S(1)}, u32[]{:S(2)}, u32[]{:S(2)}) collective-permute-start(f32[1,10,1,128]{3,2,1,0:T(1,128)S(1)} %get-tuple-element.61), channel_id=1, source_target_pairs={{1,0},{2,1},{3,2},{4,3},{5,4},{6,5},{7,6},{9,8},{10,9},{11,10},{12... | collective-permute-start | bytes 15368 | tf_op jit(solution)/shard_map/ppermute | solution.py:20
  179.8 15.8 %copy-start.3 = (f32[8,8,128]{2,1,0:T(8,128)S(1)}, f32[8,8,128]{2,1,0:T(8,128)}, u32[]{:S(2)}) copy-start(f32[8,8,128]{2,1,0:T(8,128)} %param.11) | copy-start | bytes 98308
  179.8 5.3 %collective-permute-start.8 = (f32[5,1,8,128]{3,2,1,0:T(8,128)S(1)}, f32[5,1,8,128]{3,2,1,0:T(8,128)S(1)}, u32[]{:S(2)}, u32[]{:S(2)}) collective-permute-start(f32[5,1,8,128]{3,2,1,0:T(8,128)S(1)} %get-tuple-element.40), channel_id=1, source_target_pairs={{0,8},{8,16},{16,24},{1,9},{9,17},{17,25},{2,10},{10,18},{18,26},{... | collective-permute-start | bytes 61448 | tf_op jit(solution)/shard_map/ppermute | solution.py:19
  183.2 5.1 %collective-permute-start.9 = (f32[5,1,8,128]{3,2,1,0:T(8,128)S(1)}, f32[5,1,8,128]{3,2,1,0:T(8,128)S(1)}, u32[]{:S(2)}, u32[]{:S(2)}) collective-permute-start(f32[5,1,8,128]{3,2,1,0:T(8,128)S(1)} %get-tuple-element.41), channel_id=1, source_target_pairs={{8,0},{16,8},{24,16},{9,1},{17,9},{25,17},{10,2},{18,10},{26,18},{... | collective-permute-start | bytes 61448 | tf_op jit(solution)/shard_map/ppermute | solution.py:20
  188.3 3.9 %collective-permute-start.10 = (f32[5,10,1,128]{3,2,1,0:T(1,128)S(1)}, f32[5,10,1,128]{3,2,1,0:T(1,128)S(1)}, u32[]{:S(2)}, u32[]{:S(2)}) collective-permute-start(f32[5,10,1,128]{3,2,1,0:T(1,128)S(1)} %get-tuple-element.36), channel_id=1, source_target_pairs={{0,1},{1,2},{2,3},{3,4},{4,5},{5,6},{6,7},{8,9},{9,10},{10,11},{11... | collective-permute-start | bytes 76808 | tf_op jit(solution)/shard_map/ppermute | solution.py:19
  190.9 4.6 %collective-permute-start.11 = (f32[5,10,1,128]{3,2,1,0:T(1,128)S(1)}, f32[5,10,1,128]{3,2,1,0:T(1,128)S(1)}, u32[]{:S(2)}, u32[]{:S(2)}) collective-permute-start(f32[5,10,1,128]{3,2,1,0:T(1,128)S(1)} %get-tuple-element.37), channel_id=1, source_target_pairs={{1,0},{2,1},{3,2},{4,3},{5,4},{6,5},{7,6},{9,8},{10,9},{11,10},{12... | collective-permute-start | bytes 76808 | tf_op jit(solution)/shard_map/ppermute | solution.py:20
  195.9 5.3 %collective-permute-start.12 = (f32[3,1,8,128]{3,2,1,0:T(8,128)S(1)}, f32[3,1,8,128]{3,2,1,0:T(8,128)S(1)}, u32[]{:S(2)}, u32[]{:S(2)}) collective-permute-start(f32[3,1,8,128]{3,2,1,0:T(8,128)S(1)} %get-tuple-element.46), channel_id=1, source_target_pairs={{0,8},{8,16},{16,24},{1,9},{9,17},{17,25},{2,10},{10,18},{18,26},{... | collective-permute-start | bytes 36872 | tf_op jit(solution)/shard_map/ppermute | solution.py:19
  199.3 5.0 %collective-permute-start.13 = (f32[3,1,8,128]{3,2,1,0:T(8,128)S(1)}, f32[3,1,8,128]{3,2,1,0:T(8,128)S(1)}, u32[]{:S(2)}, u32[]{:S(2)}) collective-permute-start(f32[3,1,8,128]{3,2,1,0:T(8,128)S(1)} %get-tuple-element.47), channel_id=1, source_target_pairs={{8,0},{16,8},{24,16},{9,1},{17,9},{25,17},{10,2},{18,10},{26,18},{... | collective-permute-start | bytes 36872 | tf_op jit(solution)/shard_map/ppermute | solution.py:20
  204.3 3.8 %collective-permute-start.14 = (f32[3,10,1,128]{3,2,1,0:T(1,128)S(1)}, f32[3,10,1,128]{3,2,1,0:T(1,128)S(1)}, u32[]{:S(2)}, u32[]{:S(2)}) collective-permute-start(f32[3,10,1,128]{3,2,1,0:T(1,128)S(1)} %get-tuple-element.42), channel_id=1, source_target_pairs={{0,1},{1,2},{2,3},{3,4},{4,5},{5,6},{6,7},{8,9},{9,10},{10,11},{11... | collective-permute-start | bytes 46088 | tf_op jit(solution)/shard_map/ppermute | solution.py:19
  206.8 4.5 %collective-permute-start.15 = (f32[3,10,1,128]{3,2,1,0:T(1,128)S(1)}, f32[3,10,1,128]{3,2,1,0:T(1,128)S(1)}, u32[]{:S(2)}, u32[]{:S(2)}) collective-permute-start(f32[3,10,1,128]{3,2,1,0:T(1,128)S(1)} %get-tuple-element.43), channel_id=1, source_target_pairs={{1,0},{2,1},{3,2},{4,3},{5,4},{6,5},{7,6},{9,8},{10,9},{11,10},{12... | collective-permute-start | bytes 46088 | tf_op jit(solution)/shard_map/ppermute | solution.py:20
  211.7 17.0 %copy-start.2 = (f32[8,8,128]{2,1,0:T(8,128)}, f32[8,8,128]{2,1,0:T(8,128)S(1)}, u32[]{:S(2)}) copy-start(f32[8,8,128]{2,1,0:T(8,128)S(1)} %get-tuple-element.6) | copy-start | bytes 98308
  211.8 5.3 %collective-permute-start.16 = (f32[5,1,8,128]{3,2,1,0:T(8,128)S(1)}, f32[5,1,8,128]{3,2,1,0:T(8,128)S(1)}, u32[]{:S(2)}, u32[]{:S(2)}) collective-permute-start(f32[5,1,8,128]{3,2,1,0:T(8,128)S(1)} %get-tuple-element.38), channel_id=1, source_target_pairs={{0,8},{8,16},{16,24},{1,9},{9,17},{17,25},{2,10},{10,18},{18,26},{... | collective-permute-start | bytes 61448 | tf_op jit(solution)/shard_map/ppermute | solution.py:19
  215.2 5.1 %collective-permute-start.17 = (f32[5,1,8,128]{3,2,1,0:T(8,128)S(1)}, f32[5,1,8,128]{3,2,1,0:T(8,128)S(1)}, u32[]{:S(2)}, u32[]{:S(2)}) collective-permute-start(f32[5,1,8,128]{3,2,1,0:T(8,128)S(1)} %get-tuple-element.39), channel_id=1, source_target_pairs={{8,0},{16,8},{24,16},{9,1},{17,9},{25,17},{10,2},{18,10},{26,18},{... | collective-permute-start | bytes 61448 | tf_op jit(solution)/shard_map/ppermute | solution.py:20
  220.3 5.1 %collective-permute-start.18 = (f32[5,10,1,128]{3,2,1,0:T(1,128)S(1)}, f32[5,10,1,128]{3,2,1,0:T(1,128)S(1)}, u32[]{:S(2)}, u32[]{:S(2)}) collective-permute-start(f32[5,10,1,128]{3,2,1,0:T(1,128)S(1)} %get-tuple-element.34), channel_id=1, source_target_pairs={{0,1},{1,2},{2,3},{3,4},{4,5},{5,6},{6,7},{8,9},{9,10},{10,11},{11... | collective-permute-start | bytes 76808 | tf_op jit(solution)/shard_map/ppermute | solution.py:19
  224.0 4.6 %collective-permute-start.19 = (f32[5,10,1,128]{3,2,1,0:T(1,128)S(1)}, f32[5,10,1,128]{3,2,1,0:T(1,128)S(1)}, u32[]{:S(2)}, u32[]{:S(2)}) collective-permute-start(f32[5,10,1,128]{3,2,1,0:T(1,128)S(1)} %get-tuple-element.35), channel_id=1, source_target_pairs={{1,0},{2,1},{3,2},{4,3},{5,4},{6,5},{7,6},{9,8},{10,9},{11,10},{12... | collective-permute-start | bytes 76808 | tf_op jit(solution)/shard_map/ppermute | solution.py:20
where the time goes:
time: 231 us; the launch traced here: 230 us
  other arithmetic  97.2 us (42%)
  starting transfers between devices  68 us (29%)
  waiting for transfers between devices  53.3 us (23%)
  local copies, waits for them, and re-layouts  6.92 us (3%)
    reduce_sum x1, other arithmetic, column_profile(): value_sum = jnp.sum(weight * values[..., None], axis=1)  91.5 us
    ppermute x10, starting transfers between devices, extended(): before = lax.ppermute(last, axis, up)  34.7 us
    ppermute x10, waiting for transfers between devices, extended(): after = lax.ppermute(first, axis, down)  27.8 us
    ppermute x10, starting transfers between devices, extended(): after = lax.ppermute(first, axis, down)  16.1 us
    all_to_all x1, waiting for transfers between devices, shards(): lax.all_to_all(send_buf, 'gx', split_axis=0, concat_axis=0, tiled=True)  11.7 us
    all_to_all x1, waiting for transfers between devices, shards(): lax.all_to_all(lax.all_to_all(send_buf, 'gx', split_axis=0, concat_axis=0...  9.35 us
    all_to_all x1, starting transfers between devices, shards(): lax.all_to_all(lax.all_to_all(col_buffer, 'gx', split_axis=0, concat_axis...  5.98 us
  transfers between devices with their start and end apart: 24, of which 12 were waited for; matrix products, arithmetic and copies ran while one was open for 43% of the time, Pallas kernels for 0%

commit v1 on v0

--- a/solution.py
+++ b/solution.py
@@ -7,6 +7,18 @@
 PRESS_STEP = 0.5
 VEL_STEP = 0.05
 DAMPING = 0.8
+
+
+def make_regions(array_here, d0, q_in):
+    far_arr = array_here.shape
+    known = array_here.reshape(*far_arr[:d0], q_in, far_arr[d0] // q_in, *far_arr[d0 + 1 :])
+    return jnp.moveaxis(known, d0, 0)
+
+
+def balance_fields(point, axis_no):
+    u1 = list(point.shape[1:])
+    u1[axis_no] *= point.shape[0]
+    return jnp.moveaxis(point, 0, axis_no).reshape(u1)
 
 
 def extended(x, sides, width):
@@ -184,13 +196,26 @@
         preferred_element_type=jnp.float32,
     )
     send_buf = send_buf.reshape(size_x, size_y, capacity, 2, marks)
+
+    def space_guide(tile_in, bus_axis, work_x, mine_x):
+        state_now = jax.lax.axis_size(bus_axis)
+        v1 = jax.lax.axis_index(bus_axis)
+        x_new, all_rows = (state_now, v1)
+        near = make_regions(tile_in, work_x, x_new)
+        pool = [near[all_rows]]
+        q = 1
+        while q < x_new:
+            w1 = near[(all_rows + q) % x_new]
+            w_next = jax.lax.ppermute(w1, bus_axis, [(w, (w + q) % x_new) for w in range(x_new)])
+            pool.append(w_next)
+            q = q + 1
+        aux = jnp.stack(pool)
+        near = aux[(all_rows - jnp.arange(x_new)) % x_new]
+        return balance_fields(near, mine_x)
+
     arrived, arrived_cols = (
         lax.all_to_all(
-            lax.all_to_all(send_buf, "gx", split_axis=0, concat_axis=0, tiled=True),
-            "gy",
-            split_axis=1,
-            concat_axis=1,
-            tiled=True,
+            space_guide(send_buf, "gx", 0, 0), "gy", split_axis=1, concat_axis=1, tiled=True
         ),
         lax.all_to_all(
             lax.all_to_all(col_buffer, "gx", split_axis=0, concat_axis=0, tiled=True),

time: 231 us -> 224 us (0.970)
  waiting for transfers between devices: 53.3 us -> 45.1 us
  starting transfers between devices: 68 us -> 70.6 us
    all_to_all x2 -> x1, waiting for transfers between devices: 21.1 us -> 7.91 us  [shards(): lax.all_to_all(space_guide(send_buf, 'gx', 0, 0), 'gy', split_axis=1, con...]
    all_to_all x1, waiting for transfers between devices: 0.01 us -> 5.72 us  [shards(): lax.all_to_all(col_buffer, 'gx', split_axis=0, concat_axis=0, tiled=True)]
    all_to_all x2 -> x1, starting transfers between devices: 7.06 us -> 3.56 us  [shards(): lax.all_to_all(space_guide(send_buf, 'gx', 0, 0), 'gy', split_axis=1, con...]
    ppermute x0 -> x3, starting transfers between devices: none -> 3.15 us  [space_guide(): jax.lax.ppermute(w1, bus_axis, [(w, (w + q) % x_new) for w in range(x_new)])]
    ppermute x10, starting transfers between devices: 34.7 us -> 37 us  [extended(): before = lax.ppermute(last, axis, up)]
  transfers between devices with their start and end apart: 24 -> 26, of which waited for: 12 -> 12; matrix products, arithmetic and copies ran while one was open for 43% -> 44% of each run, Pallas kernels for 0% -> 0%
where the time goes in v1:
time: 224 us; the launch traced here: 223 us
  other arithmetic  96 us (43%)
  starting transfers between devices  70.6 us (32%)
  waiting for transfers between devices  45.1 us (20%)
  local copies, waits for them, and re-layouts  7.65 us (3%)
    reduce_sum x1, other arithmetic, column_profile(): value_sum = jnp.sum(weight * values[..., None], axis=1)  91.5 us
    ppermute x10, starting transfers between devices, extended(): before = lax.ppermute(last, axis, up)  37 us
    ppermute x10, waiting for transfers between devices, extended(): after = lax.ppermute(first, axis, down)  27.8 us
    ppermute x10, starting transfers between devices, extended(): after = lax.ppermute(first, axis, down)  16.1 us
    all_to_all x1, waiting for transfers between devices, shards(): lax.all_to_all(space_guide(send_buf, 'gx', 0, 0), 'gy', split_axis=1, con...  7.91 us
    all_to_all x1, starting transfers between devices, shards(): lax.all_to_all(lax.all_to_all(col_buffer, 'gx', split_axis=0, concat_axis...  6.31 us
    all_to_all x1, waiting for transfers between devices, shards(): lax.all_to_all(col_buffer, 'gx', split_axis=0, concat_axis=0, tiled=True)  5.72 us
    all_to_all x1, starting transfers between devices, shards(): lax.all_to_all(col_buffer, 'gx', split_axis=0, concat_axis=0, tiled=True)  4.58 us
  transfers between devices with their start and end apart: 26, of which 12 were waited for; matrix products, arithmetic and copies ran while one was open for 44% of the time, Pallas kernels for 0%

profile of v1, /device:TPU:1, one launch (start us, length us, event | category | flops | bytes accessed | tf_op | source)
XLA Modules:
  0.0 222.6 jit_solution(9162652303530708692)
XLA Ops:
  6.0 2.7 %collective-permute-start = (f32[1,8,16,2,256]{4,2,3,1,0:T(8,128)S(1)}, f32[1,8,16,2,256]{4,2,3,1,0:T(8,128)S(1)}, u32[]{:S(2)}, u32[]{:S(2)}) collective-permute-start(f32[1,8,16,2,256]{4,2,3,1,0:T(8,128)S(1)} %get-tuple-element.21), channel_id=1, source_target_pairs={{0,8},{8,16},{16,24},{24,0},{1,9},{9,17},{17,25},{25,1},{2,10},{10... | collective-permute-start | bytes 786440 | tf_op jit(solution)/shard_map/ppermute | solution.py:209
  10.0 4.6 %all-to-all-start = ((s32[4,1,128]{2,1,0:T(1,128)}), s32[4,1,128]{2,1,0:T(1,128)S(1)}, u32[]{:S(2)}, u32[]{:S(2)}) async-start(s32[4,1,128]{2,1,0:T(1,128)} %reshape.244), calls=%async_computation | async-start | bytes 4096 | tf_op jit(solution)/shard_map/all_to_all | solution.py:221
  14.6 5.7 %all-to-all-done = s32[4,1,128]{2,1,0:T(1,128)S(1)} async-done(((s32[4,1,128]{2,1,0:T(1,128)}), s32[4,1,128]{2,1,0:T(1,128)S(1)}, u32[]{:S(2)}, u32[]{:S(2)}) %all-to-all-start) | async-done | bytes 2080 | tf_op jit(solution)/shard_map/all_to_all | solution.py:221
  22.2 6.3 %all-to-all-start.1 = ((s32[4,8,16]{2,0,1:T(4,128)}), s32[4,8,16]{2,0,1:T(4,128)S(1)}, u32[]{:S(2)}, u32[]{:S(2)}) async-start(s32[4,8,16]{2,0,1:T(4,128)} %copy.41), calls=%async_computation.1 | async-start | bytes 32768 | tf_op jit(solution)/shard_map/all_to_all | solution.py:220
  30.3 3.6 %all-to-all-done.1 = s32[4,8,16]{2,0,1:T(4,128)S(1)} async-done(((s32[4,8,16]{2,0,1:T(4,128)}), s32[4,8,16]{2,0,1:T(4,128)S(1)}, u32[]{:S(2)}, u32[]{:S(2)}) %all-to-all-start.1) | async-done | bytes 2080 | tf_op jit(solution)/shard_map/all_to_all | solution.py:220
  33.9 3.6 %all-to-all-start.2 = ((f32[4,8,16,2,256]{4,2,3,0,1:T(8,128)}), f32[4,8,16,2,256]{4,2,3,0,1:T(8,128)S(1)}, u32[]{:S(2)}, u32[]{:S(2)}) async-start(f32[4,8,16,2,256]{4,2,3,0,1:T(8,128)} %copy.45), calls=%async_computation.2 | async-start | bytes 2097152 | tf_op jit(solution)/shard_map/all_to_all | solution.py:217
  37.5 5.1 %collective-permute-start.7 = (f32[3,1,8,128]{3,2,1,0:T(8,128)S(1)}, f32[3,1,8,128]{3,2,1,0:T(8,128)S(1)}, u32[]{:S(2)}, u32[]{:S(2)}) collective-permute-start(f32[3,1,8,128]{3,2,1,0:T(8,128)S(1)} %get-tuple-element.53), channel_id=1, source_target_pairs={{0,8},{8,16},{16,24},{1,9},{9,17},{17,25},{2,10},{10,18},{18,26},{... | collective-permute-start | bytes 36872 | tf_op jit(solution)/shard_map/ppermute | solution.py:31
  42.6 1.9 collective-permute-start.8
  44.7 3.2 %collective-permute-done.8 = f32[3,1,8,128]{3,2,1,0:T(8,128)S(1)} collective-permute-done((f32[3,1,8,128]{3,2,1,0:T(8,128)S(1)}, f32[3,1,8,128]{3,2,1,0:T(8,128)S(1)}, u32[]{:S(2)}, u32[]{:S(2)}) %collective-permute-start.8) | collective-permute-done | bytes 12320 | tf_op jit(solution)/shard_map/ppermute | solution.py:32
  49.3 4.2 %collective-permute-start.9 = (f32[3,10,1,128]{3,2,1,0:T(1,128)S(1)}, f32[3,10,1,128]{3,2,1,0:T(1,128)S(1)}, u32[]{:S(2)}, u32[]{:S(2)}) collective-permute-start(f32[3,10,1,128]{3,2,1,0:T(1,128)S(1)} %get-tuple-element.48), channel_id=1, source_target_pairs={{0,1},{1,2},{2,3},{3,4},{4,5},{5,6},{6,7},{8,9},{9,10},{10,11},{11... | collective-permute-start | bytes 46088 | tf_op jit(solution)/shard_map/ppermute | solution.py:31
  53.4 7.9 %all-to-all-done.2 = f32[4,8,16,2,256]{4,2,3,0,1:T(8,128)S(1)} async-done(((f32[4,8,16,2,256]{4,2,3,0,1:T(8,128)}), f32[4,8,16,2,256]{4,2,3,0,1:T(8,128)S(1)}, u32[]{:S(2)}, u32[]{:S(2)}) %all-to-all-start.2) | async-done | bytes 1048608 | tf_op jit(solution)/shard_map/all_to_all | solution.py:217
  61.7 91.5 %multiply_reduce_fusion = (f32[512,128]{1,0:T(8,128)S(1)}, f32[512,128]{1,0:T(8,128)S(1)}) fusion(f32[512,256]{1,0:T(8,128)S(1)} %slice_bitcast_fusion, f32[512,256]{1,0:T(8,128)S(1)} %get-tuple-element.17, s32[512,256]{1,0:T(8,128)S(1)} %broadcast_add_fusion, f32[512,256]{1,0:T(8,128)S(1)} %get-tuple-element.16, s32[512,256]{1,0:T(8,128)S(1)} %get-tuple-element.15), kind=kLoop, calls=%fused_computation.1 | loop fusion | flops 134086656 | bytes 3145728 | tf_op jit(solution)/shard_map/reduce_sum | solution.py:75
  154.1 6.2 %collective-permute-start.3 = (f32[1,1,8,128]{3,2,1,0:T(8,128)S(1)}, f32[1,1,8,128]{3,2,1,0:T(8,128)S(1)}, u32[]{:S(2)}, u32[]{:S(2)}) collective-permute-start(f32[1,1,8,128]{3,2,1,0:T(8,128)S(1)} %get-tuple-element.66), channel_id=1, source_target_pairs={{0,8},{8,16},{16,24},{1,9},{9,17},{17,25},{2,10},{10,18},{18,26},{... | collective-permute-start | bytes 12296 | tf_op jit(solution)/shard_map/ppermute | solution.py:31
  160.3 1.9 collective-permute-start.4
  162.3 2.9 %collective-permute-done.4 = f32[1,1,8,128]{3,2,1,0:T(8,128)S(1)} collective-permute-done((f32[1,1,8,128]{3,2,1,0:T(8,128)S(1)}, f32[1,1,8,128]{3,2,1,0:T(8,128)S(1)}, u32[]{:S(2)}, u32[]{:S(2)}) %collective-permute-start.4) | collective-permute-done | bytes 4128 | tf_op jit(solution)/shard_map/ppermute | solution.py:32
  165.2 2.7 %collective-permute-start.5 = (f32[1,10,1,128]{3,2,1,0:T(1,128)S(1)}, f32[1,10,1,128]{3,2,1,0:T(1,128)S(1)}, u32[]{:S(2)}, u32[]{:S(2)}) collective-permute-start(f32[1,10,1,128]{3,2,1,0:T(1,128)S(1)} %get-tuple-element.64), channel_id=1, source_target_pairs={{0,1},{1,2},{2,3},{3,4},{4,5},{5,6},{6,7},{8,9},{9,10},{10,11},{11... | collective-permute-start | bytes 15368 | tf_op jit(solution)/shard_map/ppermute | solution.py:31
  169.4 2.9 %collective-permute-done.6 = f32[1,10,1,128]{3,2,1,0:T(1,128)S(1)} collective-permute-done((f32[1,10,1,128]{3,2,1,0:T(1,128)S(1)}, f32[1,10,1,128]{3,2,1,0:T(1,128)S(1)}, u32[]{:S(2)}, u32[]{:S(2)}) %collective-permute-start.6) | collective-permute-done | bytes 5152 | tf_op jit(solution)/shard_map/ppermute | solution.py:32
  172.9 3.4 %collective-permute-start.11 = (f32[5,1,8,128]{3,2,1,0:T(8,128)S(1)}, f32[5,1,8,128]{3,2,1,0:T(8,128)S(1)}, u32[]{:S(2)}, u32[]{:S(2)}) collective-permute-start(f32[5,1,8,128]{3,2,1,0:T(8,128)S(1)} %get-tuple-element.44), channel_id=1, source_target_pairs={{0,8},{8,16},{16,24},{1,9},{9,17},{17,25},{2,10},{10,18},{18,26},{... | collective-permute-start | bytes 61448 | tf_op jit(solution)/shard_map/ppermute | solution.py:31
  176.2 1.9 collective-permute-start.12
  178.2 3.2 %collective-permute-done.12 = f32[5,1,8,128]{3,2,1,0:T(8,128)S(1)} collective-permute-done((f32[5,1,8,128]{3,2,1,0:T(8,128)S(1)}, f32[5,1,8,128]{3,2,1,0:T(8,128)S(1)}, u32[]{:S(2)}, u32[]{:S(2)}) %collective-permute-start.12) | collective-permute-done | bytes 20512 | tf_op jit(solution)/shard_map/ppermute | solution.py:32
  181.4 2.5 %collective-permute-start.13 = (f32[5,10,1,128]{3,2,1,0:T(1,128)S(1)}, f32[5,10,1,128]{3,2,1,0:T(1,128)S(1)}, u32[]{:S(2)}, u32[]{:S(2)}) collective-permute-start(f32[5,10,1,128]{3,2,1,0:T(1,128)S(1)} %get-tuple-element.40), channel_id=1, source_target_pairs={{0,1},{1,2},{2,3},{3,4},{4,5},{5,6},{6,7},{8,9},{9,10},{10,11},{11... | collective-permute-start | bytes 76808 | tf_op jit(solution)/shard_map/ppermute | solution.py:31
  185.3 3.2 %collective-permute-done.14 = f32[5,10,1,128]{3,2,1,0:T(1,128)S(1)} collective-permute-done((f32[5,10,1,128]{3,2,1,0:T(1,128)S(1)}, f32[5,10,1,128]{3,2,1,0:T(1,128)S(1)}, u32[]{:S(2)}, u32[]{:S(2)}) %collective-permute-start.14) | collective-permute-done | bytes 25632 | tf_op jit(solution)/shard_map/ppermute | solution.py:32
  189.0 3.4 %collective-permute-start.15 = (f32[3,1,8,128]{3,2,1,0:T(8,128)S(1)}, f32[3,1,8,128]{3,2,1,0:T(8,128)S(1)}, u32[]{:S(2)}, u32[]{:S(2)}) collective-permute-start(f32[3,1,8,128]{3,2,1,0:T(8,128)S(1)} %get-tuple-element.50), channel_id=1, source_target_pairs={{0,8},{8,16},{16,24},{1,9},{9,17},{17,25},{2,10},{10,18},{18,26},{... | collective-permute-start | bytes 36872 | tf_op jit(solution)/shard_map/ppermute | solution.py:31
  192.3 1.9 collective-permute-start.16
  194.3 3.1 %collective-permute-done.16 = f32[3,1,8,128]{3,2,1,0:T(8,128)S(1)} collective-permute-done((f32[3,1,8,128]{3,2,1,0:T(8,128)S(1)}, f32[3,1,8,128]{3,2,1,0:T(8,128)S(1)}, u32[]{:S(2)}, u32[]{:S(2)}) %collective-permute-start.16) | collective-permute-done | bytes 12320 | tf_op jit(solution)/shard_map/ppermute | solution.py:32
  197.4 2.5 %collective-permute-start.17 = (f32[3,10,1,128]{3,2,1,0:T(1,128)S(1)}, f32[3,10,1,128]{3,2,1,0:T(1,128)S(1)}, u32[]{:S(2)}, u32[]{:S(2)}) collective-permute-start(f32[3,10,1,128]{3,2,1,0:T(1,128)S(1)} %get-tuple-element.46), channel_id=1, source_target_pairs={{0,1},{1,2},{2,3},{3,4},{4,5},{5,6},{6,7},{8,9},{9,10},{10,11},{11... | collective-permute-start | bytes 46088 | tf_op jit(solution)/shard_map/ppermute | solution.py:31
  201.2 3.2 %collective-permute-done.18 = f32[3,10,1,128]{3,2,1,0:T(1,128)S(1)} collective-permute-done((f32[3,10,1,128]{3,2,1,0:T(1,128)S(1)}, f32[3,10,1,128]{3,2,1,0:T(1,128)S(1)}, u32[]{:S(2)}, u32[]{:S(2)}) %collective-permute-start.18) | collective-permute-done | bytes 15392 | tf_op jit(solution)/shard_map/ppermute | solution.py:32
  204.9 3.4 %collective-permute-start.19 = (f32[5,1,8,128]{3,2,1,0:T(8,128)S(1)}, f32[5,1,8,128]{3,2,1,0:T(8,128)S(1)}, u32[]{:S(2)}, u32[]{:S(2)}) collective-permute-start(f32[5,1,8,128]{3,2,1,0:T(8,128)S(1)} %get-tuple-element.42), channel_id=1, source_target_pairs={{0,8},{8,16},{16,24},{1,9},{9,17},{17,25},{2,10},{10,18},{18,26},{... | collective-permute-start | bytes 61448 | tf_op jit(solution)/shard_map/ppermute | solution.py:31
  208.2 1.9 collective-permute-start.20
  210.2 3.2 %collective-permute-done.20 = f32[5,1,8,128]{3,2,1,0:T(8,128)S(1)} collective-permute-done((f32[5,1,8,128]{3,2,1,0:T(8,128)S(1)}, f32[5,1,8,128]{3,2,1,0:T(8,128)S(1)}, u32[]{:S(2)}, u32[]{:S(2)}) %collective-permute-start.20) | collective-permute-done | bytes 20512 | tf_op jit(solution)/shard_map/ppermute | solution.py:32
  213.4 3.7 %collective-permute-start.21 = (f32[5,10,1,128]{3,2,1,0:T(1,128)S(1)}, f32[5,10,1,128]{3,2,1,0:T(1,128)S(1)}, u32[]{:S(2)}, u32[]{:S(2)}) collective-permute-start(f32[5,10,1,128]{3,2,1,0:T(1,128)S(1)} %get-tuple-element.38), channel_id=1, source_target_pairs={{0,1},{1,2},{2,3},{3,4},{4,5},{5,6},{6,7},{8,9},{9,10},{10,11},{11... | collective-permute-start | bytes 76808 | tf_op jit(solution)/shard_map/ppermute | solution.py:31
  218.5 3.1 %collective-permute-done.22 = f32[5,10,1,128]{3,2,1,0:T(1,128)S(1)} collective-permute-done((f32[5,10,1,128]{3,2,1,0:T(1,128)S(1)}, f32[5,10,1,128]{3,2,1,0:T(1,128)S(1)}, u32[]{:S(2)}, u32[]{:S(2)}) %collective-permute-start.22) | collective-permute-done | bytes 25632 | tf_op jit(solution)/shard_map/ppermute | solution.py:32
  (136 shorter events, 20.1 us)
Async XLA Ops:
  0.6 4.5 %copy-start.7 = (s32[256]{0:T(256)S(1)}, s32[256]{0:T(256)}, u32[]{:S(2)}) copy-start(s32[256]{0:T(256)} %param.16) | copy-start | bytes 3076
  6.0 22.6 %collective-permute-start = (f32[1,8,16,2,256]{4,2,3,1,0:T(8,128)S(1)}, f32[1,8,16,2,256]{4,2,3,1,0:T(8,128)S(1)}, u32[]{:S(2)}, u32[]{:S(2)}) collective-permute-start(f32[1,8,16,2,256]{4,2,3,1,0:T(8,128)S(1)} %get-tuple-element.21), channel_id=1, source_target_pairs={{0,8},{8,16},{16,24},{24,0},{1,9},{9,17},{17,25},{25,1},{2,10},{10... | collective-permute-start | bytes 786440 | tf_op jit(solution)/shard_map/ppermute | solution.py:209
  8.6 19.9 %collective-permute-start.1 = (f32[1,8,16,2,256]{4,2,3,1,0:T(8,128)S(1)}, f32[1,8,16,2,256]{4,2,3,1,0:T(8,128)S(1)}, u32[]{:S(2)}, u32[]{:S(2)}) collective-permute-start(f32[1,8,16,2,256]{4,2,3,1,0:T(8,128)S(1)} %get-tuple-element.20), channel_id=1, source_target_pairs={{0,16},{8,24},{16,0},{24,8},{1,17},{9,25},{17,1},{25,9},{2,18},{10... | collective-permute-start | bytes 786440 | tf_op jit(solution)/shard_map/ppermute | solution.py:209
  8.6 19.9 %collective-permute-start.2 = (f32[1,8,16,2,256]{4,2,3,1,0:T(8,128)S(1)}, f32[1,8,16,2,256]{4,2,3,1,0:T(8,128)S(1)}, u32[]{:S(2)}, u32[]{:S(2)}) collective-permute-start(f32[1,8,16,2,256]{4,2,3,1,0:T(8,128)S(1)} %get-tuple-element.19), channel_id=1, source_target_pairs={{0,24},{8,0},{16,8},{24,16},{1,25},{9,1},{17,9},{25,17},{2,26},{10... | collective-permute-start | bytes 786440 | tf_op jit(solution)/shard_map/ppermute | solution.py:209
  10.0 10.3 %all-to-all-start = ((s32[4,1,128]{2,1,0:T(1,128)}), s32[4,1,128]{2,1,0:T(1,128)S(1)}, u32[]{:S(2)}, u32[]{:S(2)}) async-start(s32[4,1,128]{2,1,0:T(1,128)} %reshape.244), calls=%async_computation | async-start | bytes 4096 | tf_op jit(solution)/shard_map/all_to_all | solution.py:221
  22.2 11.7 %all-to-all-start.1 = ((s32[4,8,16]{2,0,1:T(4,128)}), s32[4,8,16]{2,0,1:T(4,128)S(1)}, u32[]{:S(2)}, u32[]{:S(2)}) async-start(s32[4,8,16]{2,0,1:T(4,128)} %copy.41), calls=%async_computation.1 | async-start | bytes 32768 | tf_op jit(solution)/shard_map/all_to_all | solution.py:220
  30.3 7.2 %copy-start = (f32[3,8,8,128]{3,2,1,0:T(8,128)S(1)}, f32[3,8,8,128]{3,2,1,0:T(8,128)}, u32[]{:S(2)}) copy-start(f32[3,8,8,128]{3,2,1,0:T(8,128)} %param.9) | copy-start | bytes 294916
  33.9 27.4 %all-to-all-start.2 = ((f32[4,8,16,2,256]{4,2,3,0,1:T(8,128)}), f32[4,8,16,2,256]{4,2,3,0,1:T(8,128)S(1)}, u32[]{:S(2)}, u32[]{:S(2)}) async-start(f32[4,8,16,2,256]{4,2,3,0,1:T(8,128)} %copy.45), calls=%async_computation.2 | async-start | bytes 2097152 | tf_op jit(solution)/shard_map/all_to_all | solution.py:217
  37.5 7.2 %collective-permute-start.7 = (f32[3,1,8,128]{3,2,1,0:T(8,128)S(1)}, f32[3,1,8,128]{3,2,1,0:T(8,128)S(1)}, u32[]{:S(2)}, u32[]{:S(2)}) collective-permute-start(f32[3,1,8,128]{3,2,1,0:T(8,128)S(1)} %get-tuple-element.53), channel_id=1, source_target_pairs={{0,8},{8,16},{16,24},{1,9},{9,17},{17,25},{2,10},{10,18},{18,26},{... | collective-permute-start | bytes 36872 | tf_op jit(solution)/shard_map/ppermute | solution.py:31
  42.6 5.3 %collective-permute-start.8 = (f32[3,1,8,128]{3,2,1,0:T(8,128)S(1)}, f32[3,1,8,128]{3,2,1,0:T(8,128)S(1)}, u32[]{:S(2)}, u32[]{:S(2)}) collective-permute-start(f32[3,1,8,128]{3,2,1,0:T(8,128)S(1)} %get-tuple-element.52), channel_id=1, source_target_pairs={{8,0},{16,8},{24,16},{9,1},{17,9},{25,17},{10,2},{18,10},{26,18},{... | collective-permute-start | bytes 36872 | tf_op jit(solution)/shard_map/ppermute | solution.py:32
  48.0 114.2 %collective-permute-start.10 = (f32[3,10,1,128]{3,2,1,0:T(1,128)S(1)}, f32[3,10,1,128]{3,2,1,0:T(1,128)S(1)}, u32[]{:S(2)}, u32[]{:S(2)}) collective-permute-start(f32[3,10,1,128]{3,2,1,0:T(1,128)S(1)} %get-tuple-element.49), channel_id=1, source_target_pairs={{1,0},{2,1},{3,2},{4,3},{5,4},{6,5},{7,6},{9,8},{10,9},{11,10},{12... | collective-permute-start | bytes 46088 | tf_op jit(solution)/shard_map/ppermute | solution.py:32
  49.3 113.0 %collective-permute-start.9 = (f32[3,10,1,128]{3,2,1,0:T(1,128)S(1)}, f32[3,10,1,128]{3,2,1,0:T(1,128)S(1)}, u32[]{:S(2)}, u32[]{:S(2)}) collective-permute-start(f32[3,10,1,128]{3,2,1,0:T(1,128)S(1)} %get-tuple-element.48), channel_id=1, source_target_pairs={{0,1},{1,2},{2,3},{3,4},{4,5},{5,6},{6,7},{8,9},{9,10},{10,11},{11... | collective-permute-start | bytes 46088 | tf_op jit(solution)/shard_map/ppermute | solution.py:31
  153.5 18.9 %copy-start.5 = (f32[8,8,128]{2,1,0:T(8,128)S(1)}, f32[8,8,128]{2,1,0:T(8,128)}, u32[]{:S(2)}) copy-start(f32[8,8,128]{2,1,0:T(8,128)} %param.10) | copy-start | bytes 98308
  154.0 18.5 %copy-start.1 = (f32[8,8,128]{2,1,0:T(8,128)}, f32[8,8,128]{2,1,0:T(8,128)S(1)}, u32[]{:S(2)}) copy-start(f32[8,8,128]{2,1,0:T(8,128)S(1)} %fusion.74) | copy-start | bytes 98308
  154.1 8.2 %collective-permute-start.3 = (f32[1,1,8,128]{3,2,1,0:T(8,128)S(1)}, f32[1,1,8,128]{3,2,1,0:T(8,128)S(1)}, u32[]{:S(2)}, u32[]{:S(2)}) collective-permute-start(f32[1,1,8,128]{3,2,1,0:T(8,128)S(1)} %get-tuple-element.66), channel_id=1, source_target_pairs={{0,8},{8,16},{16,24},{1,9},{9,17},{17,25},{2,10},{10,18},{18,26},{... | collective-permute-start | bytes 12296 | tf_op jit(solution)/shard_map/ppermute | solution.py:31
  160.3 4.9 %collective-permute-start.4 = (f32[1,1,8,128]{3,2,1,0:T(8,128)S(1)}, f32[1,1,8,128]{3,2,1,0:T(8,128)S(1)}, u32[]{:S(2)}, u32[]{:S(2)}) collective-permute-start(f32[1,1,8,128]{3,2,1,0:T(8,128)S(1)} %get-tuple-element.67), channel_id=1, source_target_pairs={{8,0},{16,8},{24,16},{9,1},{17,9},{25,17},{10,2},{18,10},{26,18},{... | collective-permute-start | bytes 12296 | tf_op jit(solution)/shard_map/ppermute | solution.py:32
  165.2 4.2 %collective-permute-start.5 = (f32[1,10,1,128]{3,2,1,0:T(1,128)S(1)}, f32[1,10,1,128]{3,2,1,0:T(1,128)S(1)}, u32[]{:S(2)}, u32[]{:S(2)}) collective-permute-start(f32[1,10,1,128]{3,2,1,0:T(1,128)S(1)} %get-tuple-element.64), channel_id=1, source_target_pairs={{0,1},{1,2},{2,3},{3,4},{4,5},{5,6},{6,7},{8,9},{9,10},{10,11},{11... | collective-permute-start | bytes 15368 | tf_op jit(solution)/shard_map/ppermute | solution.py:31
  167.9 4.4 %collective-permute-start.6 = (f32[1,10,1,128]{3,2,1,0:T(1,128)S(1)}, f32[1,10,1,128]{3,2,1,0:T(1,128)S(1)}, u32[]{:S(2)}, u32[]{:S(2)}) collective-permute-start(f32[1,10,1,128]{3,2,1,0:T(1,128)S(1)} %get-tuple-element.65), channel_id=1, source_target_pairs={{1,0},{2,1},{3,2},{4,3},{5,4},{6,5},{7,6},{9,8},{10,9},{11,10},{12... | collective-permute-start | bytes 15368 | tf_op jit(solution)/shard_map/ppermute | solution.py:32
  172.8 15.8 %copy-start.3 = (f32[8,8,128]{2,1,0:T(8,128)S(1)}, f32[8,8,128]{2,1,0:T(8,128)}, u32[]{:S(2)}) copy-start(f32[8,8,128]{2,1,0:T(8,128)} %param.11) | copy-start | bytes 98308
  172.9 5.3 %collective-permute-start.11 = (f32[5,1,8,128]{3,2,1,0:T(8,128)S(1)}, f32[5,1,8,128]{3,2,1,0:T(8,128)S(1)}, u32[]{:S(2)}, u32[]{:S(2)}) collective-permute-start(f32[5,1,8,128]{3,2,1,0:T(8,128)S(1)} %get-tuple-element.44), channel_id=1, source_target_pairs={{0,8},{8,16},{16,24},{1,9},{9,17},{17,25},{2,10},{10,18},{18,26},{... | collective-permute-start | bytes 61448 | tf_op jit(solution)/shard_map/ppermute | solution.py:31
  176.2 5.1 %collective-permute-start.12 = (f32[5,1,8,128]{3,2,1,0:T(8,128)S(1)}, f32[5,1,8,128]{3,2,1,0:T(8,128)S(1)}, u32[]{:S(2)}, u32[]{:S(2)}) collective-permute-start(f32[5,1,8,128]{3,2,1,0:T(8,128)S(1)} %get-tuple-element.45), channel_id=1, source_target_pairs={{8,0},{16,8},{24,16},{9,1},{17,9},{25,17},{10,2},{18,10},{26,18},{... | collective-permute-start | bytes 61448 | tf_op jit(solution)/shard_map/ppermute | solution.py:32
  181.4 3.9 %collective-permute-start.13 = (f32[5,10,1,128]{3,2,1,0:T(1,128)S(1)}, f32[5,10,1,128]{3,2,1,0:T(1,128)S(1)}, u32[]{:S(2)}, u32[]{:S(2)}) collective-permute-start(f32[5,10,1,128]{3,2,1,0:T(1,128)S(1)} %get-tuple-element.40), channel_id=1, source_target_pairs={{0,1},{1,2},{2,3},{3,4},{4,5},{5,6},{6,7},{8,9},{9,10},{10,11},{11... | collective-permute-start | bytes 76808 | tf_op jit(solution)/shard_map/ppermute | solution.py:31
  183.9 4.6 %collective-permute-start.14 = (f32[5,10,1,128]{3,2,1,0:T(1,128)S(1)}, f32[5,10,1,128]{3,2,1,0:T(1,128)S(1)}, u32[]{:S(2)}, u32[]{:S(2)}) collective-permute-start(f32[5,10,1,128]{3,2,1,0:T(1,128)S(1)} %get-tuple-element.41), channel_id=1, source_target_pairs={{1,0},{2,1},{3,2},{4,3},{5,4},{6,5},{7,6},{9,8},{10,9},{11,10},{12... | collective-permute-start | bytes 76808 | tf_op jit(solution)/shard_map/ppermute | solution.py:32
  189.0 5.3 %collective-permute-start.15 = (f32[3,1,8,128]{3,2,1,0:T(8,128)S(1)}, f32[3,1,8,128]{3,2,1,0:T(8,128)S(1)}, u32[]{:S(2)}, u32[]{:S(2)}) collective-permute-start(f32[3,1,8,128]{3,2,1,0:T(8,128)S(1)} %get-tuple-element.50), channel_id=1, source_target_pairs={{0,8},{8,16},{16,24},{1,9},{9,17},{17,25},{2,10},{10,18},{18,26},{... | collective-permute-start | bytes 36872 | tf_op jit(solution)/shard_map/ppermute | solution.py:31
  192.3 5.0 %collective-permute-start.16 = (f32[3,1,8,128]{3,2,1,0:T(8,128)S(1)}, f32[3,1,8,128]{3,2,1,0:T(8,128)S(1)}, u32[]{:S(2)}, u32[]{:S(2)}) collective-permute-start(f32[3,1,8,128]{3,2,1,0:T(8,128)S(1)} %get-tuple-element.51), channel_id=1, source_target_pairs={{8,0},{16,8},{24,16},{9,1},{17,9},{25,17},{10,2},{18,10},{26,18},{... | collective-permute-start | bytes 36872 | tf_op jit(solution)/shard_map/ppermute | solution.py:32
  197.4 3.8 %collective-permute-start.17 = (f32[3,10,1,128]{3,2,1,0:T(1,128)S(1)}, f32[3,10,1,128]{3,2,1,0:T(1,128)S(1)}, u32[]{:S(2)}, u32[]{:S(2)}) collective-permute-start(f32[3,10,1,128]{3,2,1,0:T(1,128)S(1)} %get-tuple-element.46), channel_id=1, source_target_pairs={{0,1},{1,2},{2,3},{3,4},{4,5},{5,6},{6,7},{8,9},{9,10},{10,11},{11... | collective-permute-start | bytes 46088 | tf_op jit(solution)/shard_map/ppermute | solution.py:31
  199.9 4.5 %collective-permute-start.18 = (f32[3,10,1,128]{3,2,1,0:T(1,128)S(1)}, f32[3,10,1,128]{3,2,1,0:T(1,128)S(1)}, u32[]{:S(2)}, u32[]{:S(2)}) collective-permute-start(f32[3,10,1,128]{3,2,1,0:T(1,128)S(1)} %get-tuple-element.47), channel_id=1, source_target_pairs={{1,0},{2,1},{3,2},{4,3},{5,4},{6,5},{7,6},{9,8},{10,9},{11,10},{12... | collective-permute-start | bytes 46088 | tf_op jit(solution)/shard_map/ppermute | solution.py:32
  204.7 17.0 %copy-start.2 = (f32[8,8,128]{2,1,0:T(8,128)}, f32[8,8,128]{2,1,0:T(8,128)S(1)}, u32[]{:S(2)}) copy-start(f32[8,8,128]{2,1,0:T(8,128)S(1)} %get-tuple-element.6) | copy-start | bytes 98308
  204.9 5.3 %collective-permute-start.19 = (f32[5,1,8,128]{3,2,1,0:T(8,128)S(1)}, f32[5,1,8,128]{3,2,1,0:T(8,128)S(1)}, u32[]{:S(2)}, u32[]{:S(2)}) collective-permute-start(f32[5,1,8,128]{3,2,1,0:T(8,128)S(1)} %get-tuple-element.42), channel_id=1, source_target_pairs={{0,8},{8,16},{16,24},{1,9},{9,17},{17,25},{2,10},{10,18},{18,26},{... | collective-permute-start | bytes 61448 | tf_op jit(solution)/shard_map/ppermute | solution.py:31
  208.2 5.1 %collective-permute-start.20 = (f32[5,1,8,128]{3,2,1,0:T(8,128)S(1)}, f32[5,1,8,128]{3,2,1,0:T(8,128)S(1)}, u32[]{:S(2)}, u32[]{:S(2)}) collective-permute-start(f32[5,1,8,128]{3,2,1,0:T(8,128)S(1)} %get-tuple-element.43), channel_id=1, source_target_pairs={{8,0},{16,8},{24,16},{9,1},{17,9},{25,17},{10,2},{18,10},{26,18},{... | collective-permute-start | bytes 61448 | tf_op jit(solution)/shard_map/ppermute | solution.py:32
  213.4 5.1 %collective-permute-start.21 = (f32[5,10,1,128]{3,2,1,0:T(1,128)S(1)}, f32[5,10,1,128]{3,2,1,0:T(1,128)S(1)}, u32[]{:S(2)}, u32[]{:S(2)}) collective-permute-start(f32[5,10,1,128]{3,2,1,0:T(1,128)S(1)} %get-tuple-element.38), channel_id=1, source_target_pairs={{0,1},{1,2},{2,3},{3,4},{4,5},{5,6},{6,7},{8,9},{9,10},{10,11},{11... | collective-permute-start | bytes 76808 | tf_op jit(solution)/shard_map/ppermute | solution.py:31
  217.1 4.6 %collective-permute-start.22 = (f32[5,10,1,128]{3,2,1,0:T(1,128)S(1)}, f32[5,10,1,128]{3,2,1,0:T(1,128)S(1)}, u32[]{:S(2)}, u32[]{:S(2)}) collective-permute-start(f32[5,10,1,128]{3,2,1,0:T(1,128)S(1)} %get-tuple-element.39), channel_id=1, source_target_pairs={{1,0},{2,1},{3,2},{4,3},{5,4},{6,5},{7,6},{9,8},{10,9},{11,10},{12... | collective-permute-start | bytes 76808 | tf_op jit(solution)/shard_map/ppermute | solution.py:32
  (2 other events, 5.2 us)
